TPU v7x, 32 devices: a whole 2x2x4 slice. The times are simulated.
32 devices in a mesh: col: 8 (over y, x, core), row: 4 (over z).
Axes of the slice: x: 2, y: 2, z: 4, core: 2. Of those that a mesh axis runs over, the one named last changes fastest.
Arguments:
- matrix: float32 [16, 512, 4096], P(None, 'row', 'col'), may hold values from -0.4 to 2.4, as said below
- pivots: int32 [8, 512], replicated, may hold values from 0 to 511, as said below
- seeds: float32 [8, 512, 512], P('col'), may hold values from -1 to 2, as said below
Outputs:
- factors: float32 [16, 512, 4096], P(None, 'row', 'col')
Inputs may be any that keep to these rules, and one draw needn't show every extreme that they name: Each row of pivots is an ordering of 0 .. 511. Block (r, j) of matrix is zero where r and j differ by more than 8. seeds[k] approximates the inverse of block (k, k) of matrix after the replacement of rows by pivots[k].
All inputs are finite; a program needn't handle non-finite values.
Results may differ from a plain program's by a relative error of at most 0.0001.
Values sent between devices are 32-bit elements; how exact they have to be, the bound alone decides.
A program may use at most 64 MiB of HBM per device.

v0:
```python
import jax
import jax.numpy as jnp
from jax import lax
from jax.sharding import PartitionSpec as P

HB = 8
SWEEPS = 2


def from_root(block, axis, source):
    block = jnp.where(lax.axis_index(axis) == source, block, jnp.zeros_like(block))
    return lax.psum(block, axis)


def dot_high(left, right):
    return jnp.dot(left, right, precision=lax.Precision.HIGHEST, preferred_element_type=jnp.float32)


def refine(pivot_block, approx, identity):
    for sweep_index in range(SWEEPS):
        approx = dot_high(approx, 2.0 * identity - dot_high(pivot_block, approx))
    return approx


def local(matrix, pivots, seeds):
    col_count = lax.axis_size("col")
    col_index = lax.axis_index("col")
    row_index = lax.axis_index("row")
    row_share = matrix.shape[1]
    panel_width = matrix.shape[2]
    identity = jnp.eye(panel_width, dtype=jnp.float32)
    seed_block = seeds[0]

    def eliminate(panel_index, factors):
        local_row = lax.dynamic_index_in_dim(factors, panel_index, 0, keepdims=False)
        block_row = lax.all_gather(local_row, "row", axis=0, tiled=True)
        ordering = lax.dynamic_index_in_dim(pivots, panel_index, 0, keepdims=False)
        swapped = jnp.take(block_row, ordering, axis=0)
        block_row = jnp.where(col_index >= panel_index, swapped, block_row)
        local_row = lax.dynamic_slice_in_dim(block_row, row_index * row_share, row_share, 0)
        factors = lax.dynamic_update_index_in_dim(factors, local_row, panel_index, 0)
        is_owner = col_index == panel_index
        approx = lax.cond(
            is_owner, lambda: refine(block_row, seed_block, identity), lambda: seed_block
        )
        below_rows = lax.dynamic_slice_in_dim(factors, panel_index + 1, HB, 0)
        below_flat = below_rows.reshape(HB * row_share, panel_width)
        scaled = lax.cond(is_owner, lambda: dot_high(below_flat, approx), lambda: below_flat)
        in_reach = (col_index > panel_index) & (col_index <= panel_index + HB)
        arrived = from_root(scaled, "col", panel_index)
        updated = below_flat - dot_high(arrived, block_row)
        result = jnp.where(is_owner, scaled, jnp.where(in_reach, updated, below_flat))
        return lax.dynamic_update_slice_in_dim(
            factors, result.reshape(HB, row_share, panel_width), panel_index + 1, 0
        )

    return lax.fori_loop(0, col_count, eliminate, matrix)


def solution(mesh):
    return jax.shard_map(
        local,
        mesh=mesh,
        in_specs=(P(None, "row", "col"), P(), P("col", None, None)),
        out_specs=P(None, "row", "col"),
        check_vma=False,
    )
```

profile of v0, /device:TPU:0, one launch (start us, length us, event | category | flops | bytes accessed | tf_op | source)
XLA Modules:
  0.0 1028.8 jit_solution(17869282881997952237)
XLA Ops:
  6.5 4.9 copy.18
  11.4 1010.8 %while.17 = (s32[]{:T(128)}, f32[16,128,512]{2,1,0:T(8,128)}, s32[]{:T(128)}, s32[8,512]{1,0:T(8,128)}, s32[]{:T(128)}, /*index=5*/f32[512,512]{1,0:T(8,128)S(1)...) while((s32[]{:T(128)}, f32[16,128,512]{2,1,0:T(8,128)}, ...), condition=%wide.region_6.7_spmd.clone.clone, body=%wide.region_0.6_spmd.clone.clone.sunk | while | flops 12889626624 | bytes 111953976 | solution.py:57
  15.0 29.5 %all-gather.6.cloned.1.call-done = f32[1,512,512]{2,1,0:T(8,128)} async-done(((f32[1,128,512]{2,1,0:T(8,128)}), f32[1,512,512]{2,1,0:T(8,128)}) %all-gather.6.cloned.1.call-update) | async-done | bytes 1048592 | tf_op jit(solution)/shard_map/while/body/eval_jaxpr/all_gather | solution.py:36
  44.5 4.1 gather_fusion
  50.7 11.3 %conditional.8 = (f32[512,512]{1,0:T(8,128)}) conditional(s32[]{:T(128)} %convert_element_type.27, f32[512,512]{1,0:T(8,128)S(1)} %get-tuple-element.345, (f32[512,512]{1,0:T(8,128)}, f32[512,512]{1,0:T(8,128)}, f32[512,512]{1,0:T(8,128)S(1)}, f32[512,512]{1,0:T(8,128)S(1)}) %tuple.77), branch_computations={%region_1.1_spmd, %region_2.2_spmd} | conditional | flops 6443499520 | bytes 18874404 | solution.py:43
  50.7 3.1 convolution_subtract_fusion
  53.8 3.5 fusion.6
  59.2 2.8 fusion.7
  63.9 6.0 conditional.9
  63.9 6.0 fusion.5
  69.9 3.1 broadcast_select_fusion.2
  73.1 59.5 %all-reduce.2.cloned.1.call-done = f32[1024,512]{1,0:T(8,128)} async-done(((f32[1024,512]{1,0:T(8,128)}), f32[1024,512]{1,0:T(8,128)}) %all-reduce.2.cloned.1.call-update) | async-done | bytes 2097168 | tf_op jit(solution)/shard_map/while/body/eval_jaxpr/psum | solution.py:12
  132.6 5.9 fusion.27
  138.8 2.0 copy-done.5
  144.4 25.8 %all-gather.6.cloned.1.call-done = f32[1,512,512]{2,1,0:T(8,128)} async-done(((f32[1,128,512]{2,1,0:T(8,128)}), f32[1,512,512]{2,1,0:T(8,128)}) %all-gather.6.cloned.1.call-update) | async-done | bytes 1048592 | tf_op jit(solution)/shard_map/while/body/eval_jaxpr/all_gather | solution.py:36
  170.2 4.1 gather_fusion
  182.2 75.3 %all-reduce.2.cloned.1.call-done = f32[1024,512]{1,0:T(8,128)} async-done(((f32[1024,512]{1,0:T(8,128)}), f32[1024,512]{1,0:T(8,128)}) %all-reduce.2.cloned.1.call-update) | async-done | bytes 2097168 | tf_op jit(solution)/shard_map/while/body/eval_jaxpr/psum | solution.py:12
  257.5 5.3 fusion.27
  263.1 2.0 copy-done.5
  268.7 25.5 %all-gather.6.cloned.1.call-done = f32[1,512,512]{2,1,0:T(8,128)} async-done(((f32[1,128,512]{2,1,0:T(8,128)}), f32[1,512,512]{2,1,0:T(8,128)}) %all-gather.6.cloned.1.call-update) | async-done | bytes 1048592 | tf_op jit(solution)/shard_map/while/body/eval_jaxpr/all_gather | solution.py:36
  294.2 4.1 gather_fusion
  306.2 76.9 %all-reduce.2.cloned.1.call-done = f32[1024,512]{1,0:T(8,128)} async-done(((f32[1024,512]{1,0:T(8,128)}), f32[1024,512]{1,0:T(8,128)}) %all-reduce.2.cloned.1.call-update) | async-done | bytes 2097168 | tf_op jit(solution)/shard_map/while/body/eval_jaxpr/psum | solution.py:12
  383.2 5.3 fusion.27
  388.7 2.0 copy-done.5
  394.4 26.3 %all-gather.6.cloned.1.call-done = f32[1,512,512]{2,1,0:T(8,128)} async-done(((f32[1,128,512]{2,1,0:T(8,128)}), f32[1,512,512]{2,1,0:T(8,128)}) %all-gather.6.cloned.1.call-update) | async-done | bytes 1048592 | tf_op jit(solution)/shard_map/while/body/eval_jaxpr/all_gather | solution.py:36
  420.6 4.1 gather_fusion
  432.6 76.5 %all-reduce.2.cloned.1.call-done = f32[1024,512]{1,0:T(8,128)} async-done(((f32[1024,512]{1,0:T(8,128)}), f32[1024,512]{1,0:T(8,128)}) %all-reduce.2.cloned.1.call-update) | async-done | bytes 2097168 | tf_op jit(solution)/shard_map/while/body/eval_jaxpr/psum | solution.py:12
  509.1 5.3 fusion.27
  514.7 2.0 copy-done.5
  520.3 25.8 %all-gather.6.cloned.1.call-done = f32[1,512,512]{2,1,0:T(8,128)} async-done(((f32[1,128,512]{2,1,0:T(8,128)}), f32[1,512,512]{2,1,0:T(8,128)}) %all-gather.6.cloned.1.call-update) | async-done | bytes 1048592 | tf_op jit(solution)/shard_map/while/body/eval_jaxpr/all_gather | solution.py:36
  546.2 4.1 gather_fusion
  558.2 76.9 %all-reduce.2.cloned.1.call-done = f32[1024,512]{1,0:T(8,128)} async-done(((f32[1024,512]{1,0:T(8,128)}), f32[1024,512]{1,0:T(8,128)}) %all-reduce.2.cloned.1.call-update) | async-done | bytes 2097168 | tf_op jit(solution)/shard_map/while/body/eval_jaxpr/psum | solution.py:12
  635.1 5.3 fusion.27
  640.7 2.0 copy-done.5
  646.3 26.3 %all-gather.6.cloned.1.call-done = f32[1,512,512]{2,1,0:T(8,128)} async-done(((f32[1,128,512]{2,1,0:T(8,128)}), f32[1,512,512]{2,1,0:T(8,128)}) %all-gather.6.cloned.1.call-update) | async-done | bytes 1048592 | tf_op jit(solution)/shard_map/while/body/eval_jaxpr/all_gather | solution.py:36
  672.6 4.1 gather_fusion
  684.6 76.5 %all-reduce.2.cloned.1.call-done = f32[1024,512]{1,0:T(8,128)} async-done(((f32[1024,512]{1,0:T(8,128)}), f32[1024,512]{1,0:T(8,128)}) %all-reduce.2.cloned.1.call-update) | async-done | bytes 2097168 | tf_op jit(solution)/shard_map/while/body/eval_jaxpr/psum | solution.py:12
  761.0 5.3 fusion.27
  766.6 2.0 copy-done.5
  772.2 25.8 %all-gather.6.cloned.1.call-done = f32[1,512,512]{2,1,0:T(8,128)} async-done(((f32[1,128,512]{2,1,0:T(8,128)}), f32[1,512,512]{2,1,0:T(8,128)}) %all-gather.6.cloned.1.call-update) | async-done | bytes 1048592 | tf_op jit(solution)/shard_map/while/body/eval_jaxpr/all_gather | solution.py:36
  798.1 4.1 gather_fusion
  810.1 77.8 %all-reduce.2.cloned.1.call-done = f32[1024,512]{1,0:T(8,128)} async-done(((f32[1024,512]{1,0:T(8,128)}), f32[1024,512]{1,0:T(8,128)}) %all-reduce.2.cloned.1.call-update) | async-done | bytes 2097168 | tf_op jit(solution)/shard_map/while/body/eval_jaxpr/psum | solution.py:12
  887.9 5.3 fusion.27
  899.1 26.2 %all-gather.6.cloned.1.call-done = f32[1,512,512]{2,1,0:T(8,128)} async-done(((f32[1,128,512]{2,1,0:T(8,128)}), f32[1,512,512]{2,1,0:T(8,128)}) %all-gather.6.cloned.1.call-update) | async-done | bytes 1048592 | tf_op jit(solution)/shard_map/while/body/eval_jaxpr/all_gather | solution.py:36
  925.3 4.1 gather_fusion
  937.3 77.4 %all-reduce.2.cloned.1.call-done = f32[1024,512]{1,0:T(8,128)} async-done(((f32[1024,512]{1,0:T(8,128)}), f32[1024,512]{1,0:T(8,128)}) %all-reduce.2.cloned.1.call-update) | async-done | bytes 2097168 | tf_op jit(solution)/shard_map/while/body/eval_jaxpr/psum | solution.py:12
  1014.7 5.3 fusion.27
  1020.3 2.0 copy-done.5
  (201 shorter events, 110.4 us)
Async XLA Ops:
  6.5 4.9 copy-start.1
  11.4 33.1 %all-gather.6.cloned.1.call-start = ((), (), s32[]{:S(2)}) async-start(), calls=%async_computation | async-start | bytes 1310720 | tf_op jit(solution)/shard_map/while/body/eval_jaxpr/all_gather | solution.py:36
  13.1 119.4 %all-reduce.2.cloned.1.call-start = ((), (), s32[]{:S(2)}) async-start(), calls=%async_computation.1 | async-start | bytes 4194304 | tf_op jit(solution)/shard_map/while/body/eval_jaxpr/psum | solution.py:12
  44.5 4.1 copy-start
  53.8 3.5 copy-start.3
  132.6 5.9 copy-start.4
  138.5 2.3 copy-start.2
  138.8 2.0 copy-start.5
  140.8 29.4 %all-gather.6.cloned.1.call-start = ((), (), s32[]{:S(2)}) async-start(), calls=%async_computation | async-start | bytes 1310720 | tf_op jit(solution)/shard_map/while/body/eval_jaxpr/all_gather | solution.py:36
  142.5 115.0 %all-reduce.2.cloned.1.call-start = ((), (), s32[]{:S(2)}) async-start(), calls=%async_computation.1 | async-start | bytes 4194304 | tf_op jit(solution)/shard_map/while/body/eval_jaxpr/psum | solution.py:12
  170.2 4.1 copy-start
  257.5 5.3 copy-start.4
  262.8 2.3 copy-start.2
  263.1 2.0 copy-start.5
  265.1 29.1 %all-gather.6.cloned.1.call-start = ((), (), s32[]{:S(2)}) async-start(), calls=%async_computation | async-start | bytes 1310720 | tf_op jit(solution)/shard_map/while/body/eval_jaxpr/all_gather | solution.py:36
  266.8 116.4 %all-reduce.2.cloned.1.call-start = ((), (), s32[]{:S(2)}) async-start(), calls=%async_computation.1 | async-start | bytes 4194304 | tf_op jit(solution)/shard_map/while/body/eval_jaxpr/psum | solution.py:12
  294.2 4.1 copy-start
  383.2 5.3 copy-start.4
  388.4 2.3 copy-start.2
  388.7 2.0 copy-start.5
  390.8 29.9 %all-gather.6.cloned.1.call-start = ((), (), s32[]{:S(2)}) async-start(), calls=%async_computation | async-start | bytes 1310720 | tf_op jit(solution)/shard_map/while/body/eval_jaxpr/all_gather | solution.py:36
  392.4 116.7 %all-reduce.2.cloned.1.call-start = ((), (), s32[]{:S(2)}) async-start(), calls=%async_computation.1 | async-start | bytes 4194304 | tf_op jit(solution)/shard_map/while/body/eval_jaxpr/psum | solution.py:12
  420.6 4.1 copy-start
  509.1 5.3 copy-start.4
  514.4 2.3 copy-start.2
  516.7 29.5 %all-gather.6.cloned.1.call-start = ((), (), s32[]{:S(2)}) async-start(), calls=%async_computation | async-start | bytes 1310720 | tf_op jit(solution)/shard_map/while/body/eval_jaxpr/all_gather | solution.py:36
  518.4 116.7 %all-reduce.2.cloned.1.call-start = ((), (), s32[]{:S(2)}) async-start(), calls=%async_computation.1 | async-start | bytes 4194304 | tf_op jit(solution)/shard_map/while/body/eval_jaxpr/psum | solution.py:12
  546.2 4.1 copy-start
  635.1 5.3 copy-start.4
  640.4 2.3 copy-start.2
  640.7 2.0 copy-start.5
  642.7 29.9 %all-gather.6.cloned.1.call-start = ((), (), s32[]{:S(2)}) async-start(), calls=%async_computation | async-start | bytes 1310720 | tf_op jit(solution)/shard_map/while/body/eval_jaxpr/all_gather | solution.py:36
  644.4 116.7 %all-reduce.2.cloned.1.call-start = ((), (), s32[]{:S(2)}) async-start(), calls=%async_computation.1 | async-start | bytes 4194304 | tf_op jit(solution)/shard_map/while/body/eval_jaxpr/psum | solution.py:12
  672.6 4.1 copy-start
  761.0 5.3 copy-start.4
  766.3 2.3 copy-start.2
  768.6 29.5 %all-gather.6.cloned.1.call-start = ((), (), s32[]{:S(2)}) async-start(), calls=%async_computation | async-start | bytes 1310720 | tf_op jit(solution)/shard_map/while/body/eval_jaxpr/all_gather | solution.py:36
  770.3 117.6 %all-reduce.2.cloned.1.call-start = ((), (), s32[]{:S(2)}) async-start(), calls=%async_computation.1 | async-start | bytes 4194304 | tf_op jit(solution)/shard_map/while/body/eval_jaxpr/psum | solution.py:12
  798.1 4.1 copy-start
  887.9 5.3 copy-start.4
  893.2 2.3 copy-start.2
  893.5 2.0 copy-start.5
  895.5 29.8 %all-gather.6.cloned.1.call-start = ((), (), s32[]{:S(2)}) async-start(), calls=%async_computation | async-start | bytes 1310720 | tf_op jit(solution)/shard_map/while/body/eval_jaxpr/all_gather | solution.py:36
  897.2 117.5 %all-reduce.2.cloned.1.call-start = ((), (), s32[]{:S(2)}) async-start(), calls=%async_computation.1 | async-start | bytes 4194304 | tf_op jit(solution)/shard_map/while/body/eval_jaxpr/psum | solution.py:12
  925.3 4.1 copy-start
  1014.7 5.3 copy-start.4
  1020.0 2.3 copy-start.2
  1020.2 2.0 copy-start.5
  (2 other events, 4.0 us)
Sparse Core Ops, SparseCore 0:
  13.8 30.6 all-gather.5
  73.2 59.3 all-reduce.1
  143.1 26.9 all-gather.5
  182.3 75.1 all-reduce.1
  267.1 27.0 all-gather.5
  306.3 76.7 all-reduce.1
  393.1 27.4 all-gather.5
  432.7 76.3 all-reduce.1
  519.1 27.0 all-gather.5
  558.3 76.7 all-reduce.1
  645.1 27.4 all-gather.5
  684.7 76.3 all-reduce.1
  771.0 27.0 all-gather.5
  810.2 77.6 all-reduce.1
  897.5 27.6 all-gather.5
  937.4 77.2 all-reduce.1
where the time goes:
time: 1030 us
  waiting for transfers between devices  808 us (78%)
  local copies, waits for them, and re-layouts  106 us (10%)
  matrix products  60 us (6%)
  other arithmetic  39.8 us (4%)
  between operations  13.1 us (1%)
    psum x8, waiting for transfers between devices, from_root(): return lax.psum(block, axis)  597 us
    all_gather x8, waiting for transfers between devices, eliminate(): block_row = lax.all_gather(local_row, 'row', axis=0, tiled=True)  211 us
    dot_general x13, matrix products, dot_high(): jnp.dot(left, right, precision=lax.Precision.HIGHEST, preferred_element_t...  60 us
    gather x8, local copies, waits for them, and re-layouts, eliminate(): swapped = jnp.take(block_row, ordering, axis=0)  32.5 us
  transfers between devices with their start and end apart: 16, of which 16 were waited for; matrix products, arithmetic and copies ran while one was open for 1% of the time, Pallas kernels for 0%

commit v1 on v0

--- a/solution.py
+++ b/solution.py
@@ -33,7 +33,14 @@
 
     def eliminate(panel_index, factors):
         local_row = lax.dynamic_index_in_dim(factors, panel_index, 0, keepdims=False)
-        block_row = lax.all_gather(local_row, "row", axis=0, tiled=True)
+        ring = [local_row]
+        for hop in range(3):
+            ring.append(lax.ppermute(ring[-1], "row", [(dev, (dev + 1) % 4) for dev in range(4)]))
+        block_row = jnp.roll(
+            jnp.concatenate(ring[::-1], axis=0),
+            (lax.axis_index("row") + 1) * ring[0].shape[0],
+            axis=0,
+        )
         ordering = lax.dynamic_index_in_dim(pivots, panel_index, 0, keepdims=False)
         swapped = jnp.take(block_row, ordering, axis=0)
         block_row = jnp.where(col_index >= panel_index, swapped, block_row)

time: 1030 us -> 970 us (0.942)
  waiting for transfers between devices: 808 us -> 740 us
  starting transfers between devices: 0.35 us -> 13.3 us
    all_gather x8 -> x0, waiting for transfers between devices: 211 us -> none  [eliminate(): block_row = lax.all_gather(local_row, 'row', axis=0, tiled=True)]
    ppermute x0 -> x24, waiting for transfers between devices: none -> 184 us  [eliminate(): lax.ppermute(ring[-1], 'row', [(dev, (dev + 1) % 4) for dev in range(4)])]
    psum x8, waiting for transfers between devices: 597 us -> 555 us  [from_root(): return lax.psum(block, axis)]
    gather x8, local copies, waits for them, and re-layouts: 32.5 us -> 18.8 us  [eliminate(): swapped = jnp.take(block_row, ordering, axis=0)]
    ppermute x0 -> x24, starting transfers between devices: none -> 13.3 us  [eliminate(): lax.ppermute(ring[-1], 'row', [(dev, (dev + 1) % 4) for dev in range(4)])]
    dynamic_slice x8, local copies, waits for them, and re-layouts: 13.4 us -> 0.55 us  [eliminate(): jnp.roll(jnp.concatenate(ring[::-1], axis=0), (lax.axis_index('row') + 1)...]
  transfers between devices with their start and end apart: 16 -> 32, of which waited for: 16 -> 32; matrix products, arithmetic and copies ran while one was open for 1% -> 1% of each run, Pallas kernels for 0% -> 0%
where the time goes in v1:
time: 970 us; the launch traced here: 968 us
  waiting for transfers between devices  740 us (76%)
  local copies, waits for them, and re-layouts  108 us (11%)
  matrix products  57.5 us (6%)
  other arithmetic  34.3 us (4%)
  between operations  13.4 us (1%)
  starting transfers between devices  13.3 us (1%)
    psum x8, waiting for transfers between devices, from_root(): return lax.psum(block, axis)  555 us
    ppermute x24, waiting for transfers between devices, eliminate(): lax.ppermute(ring[-1], 'row', [(dev, (dev + 1) % 4) for dev in range(4)])  184 us
    dot_general x13, matrix products, dot_high(): jnp.dot(left, right, precision=lax.Precision.HIGHEST, preferred_element_t...  57.5 us
  transfers between devices with their start and end apart: 32, of which 32 were waited for; matrix products, arithmetic and copies ran while one was open for 1% of the time, Pallas kernels for 0%

profile of v1, /device:TPU:0, one launch (start us, length us, event | category | flops | bytes accessed | tf_op | source)
XLA Modules:
  0.0 967.8 jit_solution(9450157458917369624)
XLA Ops:
  6.5 4.9 copy.25
  11.4 949.5 %while.17 = (s32[]{:T(128)}, f32[16,128,512]{2,1,0:T(8,128)}, s32[]{:T(128)}, s32[8,512]{1,0:T(8,128)}, s32[]{:T(128)}, /*index=5*/f32[512,512]{1,0:T(8,128)S(1)...) while((s32[]{:T(128)}, f32[16,128,512]{2,1,0:T(8,128)}, ...), condition=%wide.region_6.7_spmd.clone.clone, body=%wide.region_0.6_spmd.clone.clone.sunk | while | flops 12889626624 | bytes 83904816 | solution.py:64
  12.4 3.1 collective-permute-start
  15.5 8.3 collective-permute-done
  24.7 8.4 collective-permute-done.1
  33.2 8.3 collective-permute-done.2
  49.8 10.0 %conditional.8 = (f32[512,512]{1,0:T(8,128)}) conditional(s32[]{:T(128)} %convert_element_type.27, f32[512,512]{1,0:T(8,128)S(1)} %get-tuple-element.358, (f32[512,512]{1,0:T(8,128)S(1)}, f32[512,512]{1,0:T(8,128)S(1)}, f32[512,512]{1,0:T(8,128)S(1)}, f32[512,512]{1,0:T(8,128)S(1)}) %tuple.77), branch_computations={%region_1.1_spmd, %region_2.2_spmd} | conditional | flops 6443499520 | bytes 14680072 | solution.py:50
  51.7 3.5 fusion.6
  61.7 6.0 conditional.9
  61.8 6.0 fusion.5
  67.7 3.1 broadcast_select_fusion.2
  70.9 57.8 %all-reduce.2.cloned.1.call-done = f32[1024,512]{1,0:T(8,128)} async-done(((f32[1024,512]{1,0:T(8,128)}), f32[1024,512]{1,0:T(8,128)}) %all-reduce.2.cloned.1.call-update) | async-done | bytes 2097168 | tf_op jit(solution)/shard_map/while/body/eval_jaxpr/psum | solution.py:12
  128.7 5.7 fusion.27
  138.4 6.8 collective-permute-done
  146.0 7.3 collective-permute-done.1
  153.4 8.1 collective-permute-done.2
  175.5 67.6 %all-reduce.2.cloned.1.call-done = f32[1024,512]{1,0:T(8,128)} async-done(((f32[1024,512]{1,0:T(8,128)}), f32[1024,512]{1,0:T(8,128)}) %all-reduce.2.cloned.1.call-update) | async-done | bytes 2097168 | tf_op jit(solution)/shard_map/while/body/eval_jaxpr/psum | solution.py:12
  243.1 5.1 fusion.27
  252.2 7.9 collective-permute-done
  260.9 7.6 collective-permute-done.1
  268.6 8.1 collective-permute-done.2
  290.8 73.0 %all-reduce.2.cloned.1.call-done = f32[1024,512]{1,0:T(8,128)} async-done(((f32[1024,512]{1,0:T(8,128)}), f32[1024,512]{1,0:T(8,128)}) %all-reduce.2.cloned.1.call-update) | async-done | bytes 2097168 | tf_op jit(solution)/shard_map/while/body/eval_jaxpr/psum | solution.py:12
  363.8 5.1 fusion.27
  372.8 7.3 collective-permute-done
  380.9 7.3 collective-permute-done.1
  388.3 8.1 collective-permute-done.2
  410.5 68.8 %all-reduce.2.cloned.1.call-done = f32[1024,512]{1,0:T(8,128)} async-done(((f32[1024,512]{1,0:T(8,128)}), f32[1024,512]{1,0:T(8,128)}) %all-reduce.2.cloned.1.call-update) | async-done | bytes 2097168 | tf_op jit(solution)/shard_map/while/body/eval_jaxpr/psum | solution.py:12
  479.3 5.1 fusion.27
  488.4 7.3 collective-permute-done
  496.5 7.3 collective-permute-done.1
  503.9 8.1 collective-permute-done.2
  526.0 74.0 %all-reduce.2.cloned.1.call-done = f32[1024,512]{1,0:T(8,128)} async-done(((f32[1024,512]{1,0:T(8,128)}), f32[1024,512]{1,0:T(8,128)}) %all-reduce.2.cloned.1.call-update) | async-done | bytes 2097168 | tf_op jit(solution)/shard_map/while/body/eval_jaxpr/psum | solution.py:12
  600.0 5.1 fusion.27
  609.1 7.3 collective-permute-done
  617.2 7.3 collective-permute-done.1
  624.6 8.1 collective-permute-done.2
  646.8 68.9 %all-reduce.2.cloned.1.call-done = f32[1024,512]{1,0:T(8,128)} async-done(((f32[1024,512]{1,0:T(8,128)}), f32[1024,512]{1,0:T(8,128)}) %all-reduce.2.cloned.1.call-update) | async-done | bytes 2097168 | tf_op jit(solution)/shard_map/while/body/eval_jaxpr/psum | solution.py:12
  715.7 5.1 fusion.27
  724.7 7.3 collective-permute-done
  732.8 7.3 collective-permute-done.1
  740.2 8.1 collective-permute-done.2
  762.4 75.1 %all-reduce.2.cloned.1.call-done = f32[1024,512]{1,0:T(8,128)} async-done(((f32[1024,512]{1,0:T(8,128)}), f32[1024,512]{1,0:T(8,128)}) %all-reduce.2.cloned.1.call-update) | async-done | bytes 2097168 | tf_op jit(solution)/shard_map/while/body/eval_jaxpr/psum | solution.py:12
  837.5 5.1 fusion.27
  846.6 7.3 collective-permute-done
  854.7 7.3 collective-permute-done.1
  862.1 8.1 collective-permute-done.2
  884.3 70.0 %all-reduce.2.cloned.1.call-done = f32[1024,512]{1,0:T(8,128)} async-done(((f32[1024,512]{1,0:T(8,128)}), f32[1024,512]{1,0:T(8,128)}) %all-reduce.2.cloned.1.call-update) | async-done | bytes 2097168 | tf_op jit(solution)/shard_map/while/body/eval_jaxpr/psum | solution.py:12
  954.3 5.1 fusion.27
  (263 shorter events, 167.3 us)
Async XLA Ops:
  6.5 4.9 copy-start
  11.4 117.2 %all-reduce.2.cloned.1.call-start = ((), (), s32[]{:S(2)}) async-start(), calls=%async_computation | async-start | bytes 4194304 | tf_op jit(solution)/shard_map/while/body/eval_jaxpr/psum | solution.py:12
  12.4 11.4 %collective-permute-start = (f32[128,512]{1,0:T(8,128)S(1)}, f32[128,512]{1,0:T(8,128)S(1)}, u32[]{:S(2)}, u32[]{:S(2)}) collective-permute-start(f32[128,512]{1,0:T(8,128)S(1)} %dynamic-slice_bitcast_fusion.2), channel_id=1, source_target_pairs={{0,1},{1,2},{2,3},{3,0},{4,5},{5,6},{6,7},{7,4},{8,9},{9,10},{10,1... | collective-permute-start | bytes 786440 | tf_op jit(solution)/shard_map/while/body/eval_jaxpr/ppermute | solution.py:38
  23.8 9.3 collective-permute-start.1
  33.1 8.4 collective-permute-start.2
  43.6 1.3 copy-start.2
  134.4 1.5 copy-start.1
  135.9 107.2 %all-reduce.2.cloned.1.call-start = ((), (), s32[]{:S(2)}) async-start(), calls=%async_computation | async-start | bytes 4194304 | tf_op jit(solution)/shard_map/while/body/eval_jaxpr/psum | solution.py:12
  136.9 8.2 collective-permute-start
  145.1 8.2 collective-permute-start.1
  153.3 8.2 collective-permute-start.2
  163.6 1.3 copy-start.2
  248.2 1.5 copy-start.1
  249.7 114.0 %all-reduce.2.cloned.1.call-start = ((), (), s32[]{:S(2)}) async-start(), calls=%async_computation | async-start | bytes 4194304 | tf_op jit(solution)/shard_map/while/body/eval_jaxpr/psum | solution.py:12
  250.7 9.4 collective-permute-start
  260.1 8.5 collective-permute-start.1
  268.5 8.2 collective-permute-start.2
  368.9 1.5 copy-start.1
  370.4 108.9 %all-reduce.2.cloned.1.call-start = ((), (), s32[]{:S(2)}) async-start(), calls=%async_computation | async-start | bytes 4194304 | tf_op jit(solution)/shard_map/while/body/eval_jaxpr/psum | solution.py:12
  371.4 8.7 collective-permute-start
  380.1 8.2 collective-permute-start.1
  388.3 8.2 collective-permute-start.2
  398.6 1.3 copy-start.2
  484.4 1.5 copy-start.1
  485.9 114.1 %all-reduce.2.cloned.1.call-start = ((), (), s32[]{:S(2)}) async-start(), calls=%async_computation | async-start | bytes 4194304 | tf_op jit(solution)/shard_map/while/body/eval_jaxpr/psum | solution.py:12
  486.9 8.7 collective-permute-start
  495.6 8.2 collective-permute-start.1
  503.8 8.2 collective-permute-start.2
  514.1 1.3 copy-start.2
  605.2 1.5 copy-start.1
  606.7 109.0 %all-reduce.2.cloned.1.call-start = ((), (), s32[]{:S(2)}) async-start(), calls=%async_computation | async-start | bytes 4194304 | tf_op jit(solution)/shard_map/while/body/eval_jaxpr/psum | solution.py:12
  607.7 8.7 collective-permute-start
  616.4 8.2 collective-permute-start.1
  624.6 8.2 collective-permute-start.2
  634.8 1.3 copy-start.2
  720.8 1.5 copy-start.1
  722.3 115.3 %all-reduce.2.cloned.1.call-start = ((), (), s32[]{:S(2)}) async-start(), calls=%async_computation | async-start | bytes 4194304 | tf_op jit(solution)/shard_map/while/body/eval_jaxpr/psum | solution.py:12
  723.3 8.7 collective-permute-start
  732.0 8.2 collective-permute-start.1
  740.2 8.2 collective-permute-start.2
  750.4 1.3 copy-start.2
  842.7 1.5 copy-start.1
  844.2 110.2 %all-reduce.2.cloned.1.call-start = ((), (), s32[]{:S(2)}) async-start(), calls=%async_computation | async-start | bytes 4194304 | tf_op jit(solution)/shard_map/while/body/eval_jaxpr/psum | solution.py:12
  845.2 8.7 collective-permute-start
  853.9 8.2 collective-permute-start.1
  862.1 8.2 collective-permute-start.2
  872.3 1.3 copy-start.2
  959.5 1.5 copy-start.1
  (1 other events, 1.3 us)
Sparse Core Ops, SparseCore 0:
  71.0 57.6 all-reduce.1
  175.6 67.4 all-reduce.1
  290.9 72.8 all-reduce.1
  410.6 68.6 all-reduce.1
  526.1 73.8 all-reduce.1
  646.9 68.7 all-reduce.1
  762.5 74.9 all-reduce.1
  884.4 69.8 all-reduce.1
